TPU v7x, 32 devices: a whole 2x2x4 slice. The times are simulated.
32 devices in a mesh: ens: 2 (over x), lat: 4 (over y, core), lon: 4 (over z).
Axes of the slice: x: 2, y: 2, z: 4, core: 2. Of those that a mesh axis runs over, the one named last changes fastest.
Arguments:
- starting_state: bfloat16 [4, 222, 128, 512], P('ens', None, 'lat', 'lon'), may hold values from -6 to 6
- random_fields: bfloat16 [4, 16, 128, 512], P('ens', None, 'lat', 'lon'), may hold values from -6 to 6
- observed: float32 [6, 13, 128, 512], P(None, None, 'lat', 'lon'), may hold values from -6 to 6
- input_weight: bfloat16 [256, 222], replicated, may hold values from -0.375 to 0.375
- random_weight: bfloat16 [256, 16], replicated, may hold values from -1.5 to 1.5
- hidden_weight: bfloat16 [256, 256], replicated, may hold values from -0.375 to 0.375
- output_weight: bfloat16 [222, 256], replicated, may hold values from -0.375 to 0.375
- diffusivity: float32 [222], replicated, may hold values from 0.02 to 0.24
Outputs:
- grad_state: bfloat16 [4, 222, 128, 512], P('ens', None, 'lat', 'lon')
- grad_w_in: float32 [256, 222], replicated
- grad_w_noise: float32 [256, 16], replicated
- grad_w_mid: float32 [256, 256], replicated
- grad_w_out: float32 [222, 256], replicated
- grad_diffusivity: float32 [222], replicated
All inputs are finite; a program needn't handle non-finite values.
Results may differ from a plain program's by a relative error of at most 0.008.
Values may be sent and summed in bfloat16 or wider, within the bound.
No kernel may reach another device: no remote copies, remote signals or barrier semaphores. Data moves between devices by JAX's collectives and lax.ppermute only.
A program may use at most 128 MiB of HBM per device.

v0:
```python
import jax
import jax.numpy as jnp
from jax import lax
from jax.sharding import PartitionSpec as P

PROGNOSTIC_COUNT = 6
LEVEL_COUNT = 37
SCORED = 13
DELTA = 0.1


def with_halo(block, sides, width):
    for axis, dim in sides:
        count = lax.axis_size(axis)
        forward = [(i, i + 1) for i in range(count - 1)]
        forward.append((count - 1, 0))
        backward = [(target, source) for source, target in forward]
        low = lax.ppermute(
            lax.slice_in_dim(block, block.shape[dim] - width, None, axis=dim), axis, forward
        )
        high = lax.ppermute(lax.slice_in_dim(block, 0, width, axis=dim), axis, backward)
        block = jnp.concatenate([low, block, high], axis=dim)
    return block


def softened_slope(diff):
    return diff * lax.rsqrt(diff * diff + DELTA * DELTA)


def silu_slope(value):
    gate = jax.nn.sigmoid(value)
    return gate * (1.0 + value * (1.0 - gate))


def pole_mask(padded):
    lat_id = lax.axis_index("lat")
    lat_count = lax.axis_size("lat")
    row_ids = jnp.arange(padded.shape[2])
    dropped = (row_ids == 0) & (lat_id == 0) | (row_ids == padded.shape[2] - 1) & (
        lat_id == lat_count - 1
    )
    return padded * jnp.logical_not(dropped)[:, None].astype(padded.dtype)


def stencil(padded, field):
    return (
        padded[:, :, 2:, 1:-1]
        + padded[:, :, :-2, 1:-1]
        + padded[:, :, 1:-1, 2:]
        + padded[:, :, 1:-1, :-2]
        - 4.0 * field
    )


def on_device(
    starting_state,
    random_fields,
    observed,
    input_weight,
    random_weight,
    hidden_weight,
    output_weight,
    diffusivity,
):
    resident_members, channels, latitude_rows, longitude_columns = starting_state.shape
    cells = latitude_rows * longitude_columns
    hidden_width = hidden_weight.shape[0]
    evaluated_rows = PROGNOSTIC_COUNT * SCORED
    padded_state = pole_mask(with_halo(starting_state, (("lat", 2), ("lon", 3)), 1))
    start = starting_state.astype(jnp.float32)
    laplacian_initial = stencil(padded_state.astype(jnp.float32), start)
    stepped = start + diffusivity[None, :, None, None] * laplacian_initial
    advanced_partner = stepped.astype(jnp.bfloat16).reshape(resident_members, channels, cells)
    random_flattened = random_fields.reshape(resident_members, random_fields.shape[1], cells)
    first_preactivation = jnp.einsum(
        "hc,mcn->mhn", input_weight, advanced_partner, preferred_element_type=jnp.float32
    )
    first_preactivation = first_preactivation + jnp.einsum(
        "hk,mkn->mhn", random_weight, random_flattened, preferred_element_type=jnp.float32
    )
    first_activation = jax.nn.silu(first_preactivation).astype(jnp.bfloat16)
    second_preactivation = jnp.einsum(
        "hk,mkn->mhn", hidden_weight, first_activation, preferred_element_type=jnp.float32
    )
    second_activation = jax.nn.silu(second_preactivation).astype(jnp.bfloat16)
    w_out_scored = output_weight.reshape(PROGNOSTIC_COUNT, LEVEL_COUNT, hidden_width)[
        :, ::3
    ].reshape(evaluated_rows, hidden_width)
    advanced_evaluated = stepped.reshape(resident_members, PROGNOSTIC_COUNT, LEVEL_COUNT, cells)[
        :, :, ::3
    ].reshape(resident_members, evaluated_rows, cells)
    member_prediction = advanced_evaluated + jnp.einsum(
        "ch,mhn->mcn", w_out_scored, second_activation, preferred_element_type=jnp.float32
    )
    member_prediction = member_prediction.astype(jnp.bfloat16).reshape(
        resident_members, evaluated_rows, latitude_rows, longitude_columns
    )
    observed_target = observed.reshape(evaluated_rows, latitude_rows, longitude_columns)
    own_values = member_prediction.astype(jnp.float32)
    shard_values = lax.all_gather(member_prediction, "ens", axis=0, tiled=True).astype(jnp.float32)

    def accumulate_member(member_index, running):
        partner_member = lax.dynamic_index_in_dim(shard_values, member_index, 0, keepdims=False)
        return running + softened_slope(own_values - partner_member)

    pairwise_sum = lax.fori_loop(
        0, shard_values.shape[0], accumulate_member, jnp.zeros_like(own_values)
    )
    member_count = resident_members * lax.axis_size("ens")
    score_gradient = (
        softened_slope(own_values - observed_target[None]) - pairwise_sum / (member_count - 1.0)
    ).astype(jnp.bfloat16)
    grad_flat = score_gradient.reshape(resident_members, evaluated_rows, cells)
    out_term = jnp.einsum(
        "mcn,mhn->ch", grad_flat, second_activation, preferred_element_type=jnp.float32
    )
    back_second = jnp.einsum(
        "ch,mcn->mhn", w_out_scored, grad_flat, preferred_element_type=jnp.float32
    )
    delta_second = (back_second * silu_slope(second_preactivation)).astype(jnp.bfloat16)
    mid_term = jnp.einsum(
        "mhn,mkn->hk", delta_second, first_activation, preferred_element_type=jnp.float32
    )
    back_first = jnp.einsum(
        "hk,mhn->mkn", hidden_weight, delta_second, preferred_element_type=jnp.float32
    )
    delta_first = (back_first * silu_slope(first_preactivation)).astype(jnp.bfloat16)
    in_term = jnp.einsum(
        "mhn,mcn->hc", delta_first, advanced_partner, preferred_element_type=jnp.float32
    )
    noise_term = jnp.einsum(
        "mhn,mkn->hk", delta_first, random_flattened, preferred_element_type=jnp.float32
    )
    grad_stepped = jnp.einsum(
        "hc,mhn->mcn", input_weight, delta_first, preferred_element_type=jnp.float32
    )
    grad_stepped = (
        grad_stepped.reshape(resident_members, PROGNOSTIC_COUNT, LEVEL_COUNT, cells)
        .at[:, :, ::3]
        .add(
            grad_flat.astype(jnp.float32).reshape(resident_members, PROGNOSTIC_COUNT, SCORED, cells)
        )
    )
    grad_stepped = grad_stepped.reshape(
        resident_members, channels, latitude_rows, longitude_columns
    )
    diffusivity_term = jnp.sum(grad_stepped * laplacian_initial, axis=(0, 2, 3))
    in_term, noise_term, mid_term, out_term, diffusivity_term = lax.psum(
        (in_term, noise_term, mid_term, out_term, diffusivity_term), ("ens", "lat", "lon")
    )
    padded_grad = pole_mask(
        with_halo(grad_stepped.astype(jnp.bfloat16), (("lat", 2), ("lon", 3)), 1).astype(
            grad_stepped.dtype
        )
    )
    grad_laplace = stencil(padded_grad, grad_stepped)
    grad_state = (grad_stepped + diffusivity[None, :, None, None] * grad_laplace).astype(
        jnp.bfloat16
    )
    inverse_count = 1.0 / (
        resident_members
        * lax.axis_size("ens")
        * latitude_rows
        * lax.axis_size("lat")
        * longitude_columns
        * lax.axis_size("lon")
    )
    grad_w_out = (
        jnp.zeros((PROGNOSTIC_COUNT, LEVEL_COUNT, hidden_width), jnp.float32)
        .at[:, ::3]
        .set(out_term.reshape(PROGNOSTIC_COUNT, SCORED, hidden_width))
        .reshape(channels, hidden_width)
    )
    return (
        grad_state,
        in_term * inverse_count,
        noise_term * inverse_count,
        mid_term * inverse_count,
        grad_w_out * inverse_count,
        diffusivity_term * inverse_count,
    )


def solution(mesh):
    in_specs = (
        P("ens", None, "lat", "lon"),
        P("ens", None, "lat", "lon"),
        P(None, None, "lat", "lon"),
        P(),
        P(),
        P(),
        P(),
        P(),
    )
    out_specs = (P("ens", None, "lat", "lon"), P(), P(), P(), P(), P())
    return jax.shard_map(
        on_device, mesh=mesh, in_specs=in_specs, out_specs=out_specs, check_vma=False
    )
```

profile of v0, /device:TPU:0, one launch (start us, length us, event | category | flops | bytes accessed | tf_op | source)
XLA Modules:
  0.0 457.5 jit_solution(17218860512130126049)
XLA Ops:
  7.2 1.9 fusion.34
  9.7 2.0 collective-permute-start.1
  11.7 1.1 reshape.82
  12.8 5.2 %fusion.27 = f32[2,4096,256]{2,1,0:T(8,128)} fusion(bf16[2,16,4096]{2,1,0:T(8,128)(2,1)S(1)} %reshape.82, bf16[256,16]{0,1:T(8,128)(2,1)} %param.14), kind=kOutput, calls=%fused_computation.67 | convolution fusion | flops 67108864 | bytes 8658944 | tf_op jit(solution)/shard_map/hk,mkn->mhn/dot_general | solution.py:78
  18.0 8.3 %copy.76 = bf16[2,222,32,128]{1,2,3,0:T(8,128)(2,1)} copy(bf16[2,222,32,128]{3,2,1,0:T(8,128)(2,1)} %param.10) | data formatting | bytes 7274496 | tf_op args[0]
  26.7 0.8 pad_maximum_fusion.5
  27.5 2.4 collective-permute-start.2
  29.9 2.4 collective-permute-start.3
  32.5 1.6 collective-permute-done.2
  34.5 4.8 %fusion.19 = f32[2,222,34,130]{1,2,3,0:T(8,128)S(1)} fusion(bf16[2,222,34,1]{1,2,3,0:T(8,128)(2,1)S(1)} %collective-permute-done.3, bf16[2,222,1,128]{1,2,3,0:T(2,128)(2,1)S(1)} %copy.81, bf16[2,222,32,128]{1,2,3,0:T(8,128)(2,1)} %copy.76, bf16[2,222,1,128]{1,2,3,0:T(2,128)(2,1)S(1)} %copy.79, bf16[2,222,34,1]{1,2,3,0:T(8,128)(2,1)S(1)} %collective-permute-done.2, ...), kind=kLoop, calls=%fused_computation.44 | loop fusion | flops 23549760 | bytes 11774948 | tf_op jit(solution)/shard_map/convert_element_type | solution.py:71
  39.3 11.2 %fusion.31 = (bf16[2,222,32,128]{1,2,3,0:T(8,128)(2,1)}, f32[2,222,32,128]{1,2,3,0:T(8,128)}, f32[2,222,32,128]{1,2,3,0:T(8,128)}) fusion(f32[222]{0:T(256)S(1)} %copy-done.10, bf16[2,222,32,128]{1,2,3,0:T(8,128)(2,1)} %copy.76, f32[2,222,34,130]{1,2,3,0:T(8,128)S(1)} %fusion.19), kind=kLoop, calls=%fused_computation.75 | loop fusion | flops 16367616 | bytes 50922360 | tf_op jit(solution)/shard_map/convert_element_type | solution.py:73
  50.5 8.3 %copy.83 = bf16[2,222,32,128]{3,2,1,0:T(8,128)(2,1)} copy(bf16[2,222,32,128]{1,2,3,0:T(8,128)(2,1)} %get-tuple-element.126) | data formatting | bytes 7274496 | tf_op jit(solution)/shard_map/convert_element_type | solution.py:73
  58.8 4.4 reshape.81
  63.2 10.1 %copy.82 = f32[2,222,32,128]{3,2,0,1:T(8,128)} copy(f32[2,222,32,128]{1,2,3,0:T(8,128)} %get-tuple-element.127) | data formatting | bytes 14548992 | tf_op jit(solution)/shard_map/add | solution.py:72
  73.3 10.0 %reshape.79 = f32[2,6,37,4096]{3,0,2,1:T(2,128)} reshape(f32[2,222,32,128]{3,2,0,1:T(8,128)} %copy.82) | data formatting | bytes 14548992 | tf_op jit(solution)/shard_map/reshape | solution.py:89
  83.3 2.0 slice.62
  85.4 9.0 %fusion.16 = (bf16[2,256,4096]{1,2,0:T(8,128)(2,1)S(1)}, f32[2,4096,256]{2,1,0:T(8,128)}) fusion(f32[2,4096,256]{2,1,0:T(8,128)} %fusion.27, bf16[2,222,4096]{2,1,0:T(8,128)(2,1)} %reshape.81, bf16[256,222]{0,1:T(8,128)(2,1)S(1)} %copy-done.8), kind=kOutput, calls=%fused_computation.37 | convolution fusion | flops 943718400 | bytes 24722432 | tf_op jit(solution)/shard_map/hc,mcn->mhn/dot_general | solution.py:75
  94.4 4.7 %fusion.10 = (bf16[2,256,4096]{1,2,0:T(8,128)(2,1)S(1)}, f32[2,4096,256]{2,1,0:T(8,128)}) fusion(bf16[2,256,4096]{1,2,0:T(8,128)(2,1)S(1)} %get-tuple-element.139, bf16[256,256]{1,0:T(8,128)(2,1)S(1)} %copy-done), kind=kOutput, calls=%fused_computation.28 | convolution fusion | flops 1084227584 | bytes 16908288 | tf_op jit(solution)/shard_map/hk,mkn->mhn/dot_general | solution.py:82
  99.1 2.0 copy-done.3
  101.1 2.0 fusion.21
  103.1 1.6 reshape.85
  105.3 3.2 convert_element_type.74
  108.5 36.1 %all-gather.2.cloned.1.call-done = bf16[4,78,32,128]{3,2,1,0:T(8,128)(2,1)} async-done(((bf16[2,78,32,128]{3,2,1,0:T(8,128)(2,1)}), bf16[4,78,32,128]{3,2,1,0:T(8,128)(2,1)}) %all-gather.2.cloned.1.call-update) | async-done | bytes 2555920 | tf_op jit(solution)/shard_map/all_gather | solution.py:100
  144.6 4.8 %convert_element_type.75 = f32[4,78,32,128]{3,2,1,0:T(8,128)} convert(bf16[4,78,32,128]{3,2,1,0:T(8,128)(2,1)} %all-gather.2.cloned.1.call-done) | non-fusion elementwise | flops 1277952 | bytes 7667712 | tf_op jit(solution)/shard_map/convert_element_type | solution.py:100
  149.4 24.0 %while.14 = (s32[]{:T(128)}, f32[2,78,32,128]{3,2,1,0:T(8,128)}, f32[4,78,32,128]{3,2,1,0:T(8,128)}, f32[2,78,32,128]{3,2,1,0:T(8,128)}, s32[]{:T(128)}, /*index=5*/s32[]{:T(128)}) while((s32[]{:T(128)}, f32[2,78,32,128]{3,2,1,0:T(8,128)}, f32[4,78,32,128]{3,2,1,0:T(8,128)}, f32[2,78,32,128]{3,2,1,0:T(8,128)}, s32[]{:T(128)}, ...), condition=%wide.region_1.2_spmd.clone, body=%wide.region_0.1_spmd.clone.sunk | while | flops 3833859 | bytes 11501651 | solution.py:106
  149.4 1.5 dynamic-slice_bitcast_fusion.2
  150.9 4.0 select_add_fusion.2
  154.9 1.4 dynamic-slice_bitcast_fusion.2
  156.3 4.8 %select_add_fusion.2 = f32[2,78,32,128]{3,2,1,0:T(8,128)} fusion(f32[2,78,32,128]{3,2,1,0:T(8,128)} %get-tuple-element.175, f32[2,78,32,128]{3,2,1,0:T(8,128)} %get-tuple-element.183, f32[78,32,128]{2,1,0:T(8,128)S(1)} %dynamic-slice_bitcast_fusion.2, pred[]{:T(512)S(6)} %compare.3), kind=kLoop, calls=%fused_computation.2.clone.1 | loop fusion | flops 3833856 | bytes 8945665 | tf_op jit(solution)/shard_map/while/body/eval_jaxpr/add | solution.py:104
  161.1 1.4 dynamic-slice_bitcast_fusion.2
  162.5 4.8 %select_add_fusion.2 = f32[2,78,32,128]{3,2,1,0:T(8,128)} fusion(f32[2,78,32,128]{3,2,1,0:T(8,128)} %get-tuple-element.175, f32[2,78,32,128]{3,2,1,0:T(8,128)} %get-tuple-element.183, f32[78,32,128]{2,1,0:T(8,128)S(1)} %dynamic-slice_bitcast_fusion.2, pred[]{:T(512)S(6)} %compare.3), kind=kLoop, calls=%fused_computation.2.clone.1 | loop fusion | flops 3833856 | bytes 8945665 | tf_op jit(solution)/shard_map/while/body/eval_jaxpr/add | solution.py:104
  167.3 1.4 dynamic-slice_bitcast_fusion.2
  168.7 4.8 %select_add_fusion.2 = f32[2,78,32,128]{3,2,1,0:T(8,128)} fusion(f32[2,78,32,128]{3,2,1,0:T(8,128)} %get-tuple-element.175, f32[2,78,32,128]{3,2,1,0:T(8,128)} %get-tuple-element.183, f32[78,32,128]{2,1,0:T(8,128)S(1)} %dynamic-slice_bitcast_fusion.2, pred[]{:T(512)S(6)} %compare.3), kind=kLoop, calls=%fused_computation.2.clone.1 | loop fusion | flops 3833856 | bytes 8945665 | tf_op jit(solution)/shard_map/while/body/eval_jaxpr/add | solution.py:104
  173.4 2.8 subtract_convert_fusion
  177.0 3.2 convolution_bitcast_fusion.4
  180.2 6.4 %fusion.6 = bf16[2,256,4096]{1,2,0:T(8,128)(2,1)S(1)} fusion(f32[2,4096,256]{2,1,0:T(8,128)} %get-tuple-element.142, bf16[2,78,4096]{2,1,0:T(8,128)(2,1)S(1)} %reshape.86, bf16[78,256,1]{1,0,2:T(8,128)(2,1)S(1)} %reshape.110), kind=kOutput, calls=%fused_computation.21 | convolution fusion | flops 346030080 | bytes 13900800 | tf_op jit(solution)/shard_map/ch,mcn->mhn/dot_general | solution.py:117
  186.6 2.0 convolution_bitcast_fusion.2
  188.6 3.5 fusion.5
  192.2 1.8 convolution_bitcast_fusion.3
  194.0 4.4 convolution_bitcast_fusion
  198.4 1.8 copy.88
  200.9 11.8 %copy.87 = f32[2,222,4096]{2,0,1:T(2,128)} copy(f32[2,222,4096]{2,1,0:T(8,128)} %convolution_bitcast_fusion) | data formatting | bytes 14548992 | tf_op jit(solution)/shard_map/hc,mhn->mcn/transpose | solution.py:134
  212.7 2.4 reshape.92
  215.1 1.9 copy.89
  217.0 16.4 %scatter_fusion = f32[2,6,37,4096]{3,0,2,1:T(2,128)} fusion(f32[2,6,37,4096]{3,0,2,1:T(2,128)} %bitcast.129, s32[13]{0:T(128)S(1)} %multiply_bitcast_fusion, f32[13,2,6,4096]{3,1,2,0:T(2,128)S(1)} %copy.89), kind=kCustom, calls=%fused_computation | custom fusion | flops 638976 | bytes 7667764 | tf_op jit(solution)/shard_map/scatter-add | solution.py:140
  233.4 10.9 %reshape.88 = f32[2,222,32,128]{3,2,0,1:T(8,128)} reshape(f32[2,6,37,4096]{3,0,2,1:T(2,128)} %scatter_fusion) | data formatting | bytes 14548992 | tf_op jit(solution)/shard_map/reshape | solution.py:144
  244.3 10.1 %copy.96 = f32[2,222,32,128]{1,2,3,0:T(8,128)} copy(f32[2,222,32,128]{3,2,0,1:T(8,128)} %reshape.88) | data formatting | bytes 14548992 | tf_op jit(solution)/shard_map/reshape | solution.py:144
  254.4 10.2 %multiply_reduce_fusion = (f32[222]{0:T(256)S(1)}, bf16[2,222,32,128]{1,2,3,0:T(8,128)(2,1)S(1)}) fusion(f32[2,222,32,128]{1,2,3,0:T(8,128)} %copy.96, f32[2,222,32,128]{1,2,3,0:T(8,128)} %get-tuple-element.128), kind=kLoop, calls=%fused_computation.40 | loop fusion | flops 5455650 | bytes 18187128 | tf_op jit(solution)/shard_map/reduce_sum | solution.py:147
  264.6 2.0 copy-done.1
  267.4 1.8 collective-permute-start.5
  269.2 39.4 %all-reduce = (f32[256,16]{0,1:T(8,128)S(1)}, f32[222]{0:T(256)S(1)}) all-reduce(f32[256,16]{0,1:T(8,128)S(1)} %convolution_bitcast_fusion.5, f32[222]{0:T(256)S(1)} %get-tuple-element.129), channel_id=1, replica_groups=mesh['ens'=2,'lat'=4,'lon'=4] {'ens','lat','lon'}, use_global_device_ids=true, to_apply=%region_4.5 | all-reduce | flops 4318 | bytes 34544 | tf_op jit(solution)/shard_map/psum | solution.py:148
  309.6 0.8 pad_maximum_fusion.2
  310.5 1.5 collective-permute-start.6
  312.0 2.4 collective-permute-start.7
  314.9 0.7 copy.102
  315.6 0.8 collective-permute-done.6
  316.4 8.6 %convert_multiply_fusion = f32[2,222,34,130]{1,2,3,0:T(8,128)} fusion(bf16[2,222,34,1]{1,2,3,0:T(8,128)(2,1)S(1)} %collective-permute-done.7, bf16[2,222,1,128]{1,2,3,0:T(2,128)(2,1)S(1)} %copy.94, bf16[2,222,32,128]{1,2,3,0:T(8,128)(2,1)} %copy-done.1, bf16[2,222,1,128]{1,2,3,0:T(2,128)(2,1)S(1)} %copy.93, ...), kind=kLoop, calls=%fused_computation.4 | loop fusion | flops 21587280 | bytes 11775016 | tf_op jit(solution)/shard_map/mul | solution.py:42
  325.0 19.3 %fusion.4 = bf16[2,222,32,128]{1,2,3,0:T(8,128)(2,1)} fusion(f32[2,222,32,128]{1,2,3,0:T(8,128)} %copy.96, f32[2,222,34,130]{1,2,3,0:T(8,128)} %convert_multiply_fusion, f32[222]{0:T(256)S(1)} %copy-done.10), kind=kLoop, calls=%fused_computation.12 | loop fusion | flops 14548992 | bytes 40010616 | tf_op jit(solution)/shard_map/convert_element_type | solution.py:157
  344.3 8.3 %copy.105 = bf16[2,222,32,128]{3,2,1,0:T(8,128)(2,1)} copy(bf16[2,222,32,128]{1,2,3,0:T(8,128)(2,1)} %fusion.4) | data formatting | bytes 7274496
  352.6 92.1 %all-reduce.4.cloned.1.call-done = (f32[256,222]{0,1:T(8,128)}, f32[256,256]{1,0:T(8,128)}, f32[6,13,256]{2,0,1:T(8,128)}) async-done(((f32[256,222]{0,1:T(8,128)}, f32[256,256]{1,0:T(8,128)}, f32[6,13,256]{2,0,1:T(8,128)}), (f32[256,222]{0,1:T(8,128)}, f32[256,256]{1,0:T(8,128)}, f32[6,13,256]{2,0,1:T(8,128)})) %all-reduce.4.cloned.1.call-update) | async-done | bytes 569360 | tf_op jit(solution)/shard_map/psum | solution.py:148
  444.7 1.7 scatter_fusion.1
  446.4 0.7 mul.158
  447.2 1.7 broadcast_multiply_fusion
  448.8 1.6 broadcast_multiply_fusion.1
  (60 shorter events, 6.1 us)
Async XLA Ops:
  7.2 87.2 %copy-start = (bf16[256,256]{1,0:T(8,128)(2,1)S(1)}, bf16[256,256]{1,0:T(8,128)(2,1)}, u32[]{:S(2)}) copy-start(bf16[256,256]{1,0:T(8,128)(2,1)} %param.15) | copy-start | bytes 393220
  7.2 137.4 %all-gather.2.cloned.1.call-start = ((), (), s32[]{:S(2)}) async-start(), calls=%async_computation | async-start | bytes 3833856 | tf_op jit(solution)/shard_map/all_gather | solution.py:100
  9.1 17.2 %collective-permute-start = (bf16[2,222,1,128]{3,1,2,0:T(8,128)(2,1)S(1)}, bf16[2,222,1,128]{3,1,2,0:T(8,128)(2,1)S(1)}, u32[]{:S(2)}, u32[]{:S(2)}) collective-permute-start(bf16[2,222,1,128]{3,1,2,0:T(8,128)(2,1)S(1)} %copy.113), channel_id=1, source_target_pairs={{0,4},{4,8},{8,12},{12,0},{1,5},{5,9},{9,13},{13,1},{2,6},{6,10},{... | collective-permute-start | bytes 341000 | tf_op jit(solution)/shard_map/ppermute | solution.py:18
  9.7 16.8 %collective-permute-start.1 = (bf16[2,222,1,128]{3,1,2,0:T(8,128)(2,1)S(1)}, bf16[2,222,1,128]{3,1,2,0:T(8,128)(2,1)S(1)}, u32[]{:S(2)}, u32[]{:S(2)}) collective-permute-start(bf16[2,222,1,128]{3,1,2,0:T(8,128)(2,1)S(1)} %copy.114), channel_id=1, source_target_pairs={{4,0},{8,4},{12,8},{0,12},{5,1},{9,5},{13,9},{1,13},{6,2},{10,6},{... | collective-permute-start | bytes 341000 | tf_op jit(solution)/shard_map/ppermute | solution.py:21
  18.0 14.3 %copy-start.9 = (bf16[222,256]{1,0:T(8,128)(2,1)S(1)}, bf16[222,256]{1,0:T(8,128)(2,1)}, u32[]{:S(2)}) copy-start(bf16[222,256]{1,0:T(8,128)(2,1)} %param.16) | copy-start | bytes 340996
  27.5 6.5 %collective-permute-start.2 = (bf16[2,222,34,1]{1,2,3,0:T(8,128)(2,1)S(1)}, bf16[2,222,34,1]{1,2,3,0:T(8,128)(2,1)S(1)}, u32[]{:S(2)}, u32[]{:S(2)}) collective-permute-start(bf16[2,222,34,1]{1,2,3,0:T(8,128)(2,1)S(1)} %get-tuple-element.133), channel_id=1, source_target_pairs={{0,1},{1,2},{2,3},{3,0},{4,5},{5,6},{6,7},{7,4},{8,9},{9,10},{10,1... | collective-permute-start | bytes 90584 | tf_op jit(solution)/shard_map/ppermute | solution.py:18
  29.9 4.5 collective-permute-start.3
  32.4 6.8 %copy-start.10 = (f32[222]{0:T(256)S(1)}, f32[222]{0:T(256)}, u32[]{:S(2)}) copy-start(f32[222]{0:T(256)} %param.17) | copy-start | bytes 2668
  73.3 12.0 %copy-start.8 = (bf16[256,222]{0,1:T(8,128)(2,1)S(1)}, bf16[256,222]{0,1:T(8,128)(2,1)}, u32[]{:S(2)}) copy-start(bf16[256,222]{0,1:T(8,128)(2,1)} %param.13) | copy-start | bytes 340996
  94.4 4.7 %copy-start.4 = (bf16[2,256,4096]{1,2,0:T(8,128)(2,1)}, bf16[2,256,4096]{1,2,0:T(8,128)(2,1)S(1)}, u32[]{:S(2)}) copy-start(bf16[2,256,4096]{1,2,0:T(8,128)(2,1)S(1)} %get-tuple-element.139) | copy-start | bytes 12582916
  99.1 2.0 copy-start.3
  104.7 339.9 %all-reduce.4.cloned.1.call-start = ((), (), s32[]{:S(2)}) async-start(), calls=%async_computation.1 | async-start | bytes 1196032 | tf_op jit(solution)/shard_map/psum | solution.py:148
  149.4 24.0 %copy-start.2 = (bf16[2,78,32,128]{3,2,1,0:T(8,128)(2,1)S(1)}, bf16[2,78,32,128]{3,2,1,0:T(8,128)(2,1)}, u32[]{:S(2)}) copy-start(bf16[2,78,32,128]{3,2,1,0:T(8,128)(2,1)} %reshape.85) | copy-start | bytes 3833860
  177.0 11.7 %slice-start = ((s8[8388608]{0:T(1024)(128)(4,1)}), s8[4194304]{0:T(1024)(128)(4,1)S(1)}, s32[]{:S(2)}) async-start(s8[8388608]{0:T(1024)(128)(4,1)} %bitcast.134), calls=%async_computation.2 | async-start | bytes 8388608
  180.2 6.5 %copy-start.5 = (bf16[2,256,4096]{1,2,0:T(8,128)(2,1)S(1)}, bf16[2,256,4096]{1,2,0:T(8,128)(2,1)}, u32[]{:S(2)}) copy-start(bf16[2,256,4096]{1,2,0:T(8,128)(2,1)} %copy-done.4) | copy-start | bytes 12582916
  180.2 8.5 %slice-start.1 = ((s8[8388608]{0:T(1024)(128)(4,1)}), s8[4194304]{0:T(1024)(128)(4,1)S(1)}, s32[]{:S(2)}) async-start(s8[8388608]{0:T(1024)(128)(4,1)} %bitcast.134), calls=%async_computation.3 | async-start | bytes 8388608
  188.6 3.6 copy-start.7
  200.9 11.8 %copy-start.6 = (f32[2,78,32,128]{3,2,0,1:T(8,128)S(1)}, f32[2,78,32,128]{3,2,0,1:T(8,128)}, u32[]{:S(2)}) copy-start(f32[2,78,32,128]{3,2,0,1:T(8,128)} %copy.88) | copy-start | bytes 7667716
  264.6 2.0 copy-start.1
  267.2 42.1 %collective-permute-start.4 = (bf16[2,222,1,128]{3,1,2,0:T(8,128)(2,1)S(1)}, bf16[2,222,1,128]{3,1,2,0:T(8,128)(2,1)S(1)}, u32[]{:S(2)}, u32[]{:S(2)}) collective-permute-start(bf16[2,222,1,128]{3,1,2,0:T(8,128)(2,1)S(1)} %copy.91), channel_id=1, source_target_pairs={{0,4},{4,8},{8,12},{12,0},{1,5},{5,9},{9,13},{13,1},{2,6},{6,10},{... | collective-permute-start | bytes 341000 | tf_op jit(solution)/shard_map/ppermute | solution.py:18
  267.4 42.0 %collective-permute-start.5 = (bf16[2,222,1,128]{3,1,2,0:T(8,128)(2,1)S(1)}, bf16[2,222,1,128]{3,1,2,0:T(8,128)(2,1)S(1)}, u32[]{:S(2)}, u32[]{:S(2)}) collective-permute-start(bf16[2,222,1,128]{3,1,2,0:T(8,128)(2,1)S(1)} %copy.92), channel_id=1, source_target_pairs={{4,0},{8,4},{12,8},{0,12},{5,1},{9,5},{13,9},{1,13},{6,2},{10,6},{... | collective-permute-start | bytes 341000 | tf_op jit(solution)/shard_map/ppermute | solution.py:21
  310.5 6.0 %collective-permute-start.6 = (bf16[2,222,34,1]{1,2,3,0:T(8,128)(2,1)S(1)}, bf16[2,222,34,1]{1,2,3,0:T(8,128)(2,1)S(1)}, u32[]{:S(2)}, u32[]{:S(2)}) collective-permute-start(bf16[2,222,34,1]{1,2,3,0:T(8,128)(2,1)S(1)} %get-tuple-element.131), channel_id=1, source_target_pairs={{0,1},{1,2},{2,3},{3,0},{4,5},{5,6},{6,7},{7,4},{8,9},{9,10},{10,1... | collective-permute-start | bytes 90584 | tf_op jit(solution)/shard_map/ppermute | solution.py:18
  312.0 4.4 collective-permute-start.7
Sparse Core Ops, SparseCore 0:
  104.9 39.6 all-gather.1
  315.8 128.8 all-reduce.3
where the time goes:
time: 463 us; the launch traced here: 458 us
  waiting for transfers between devices  131 us (28%)
  local copies, waits for them, and re-layouts  110 us (24%)
  other arithmetic  106 us (23%)
  matrix products  43 us (9%)
  blocking collectives  39.4 us (9%)
  between operations  14.6 us (3%)
  starting transfers between devices  13.7 us (3%)
    psum x1, waiting for transfers between devices, on_device(): lax.psum((in_term, noise_term, mid_term, out_term, diffusivity_term), ('e...  92.1 us
    psum x1, blocking collectives, on_device(): lax.psum((in_term, noise_term, mid_term, out_term, diffusivity_term), ('e...  39.4 us
    all_gather x1, waiting for transfers between devices, on_device(): lax.all_gather(member_prediction, 'ens', axis=0, tiled=True)  36.1 us
    reshape x2, local copies, waits for them, and re-layouts, on_device(): grad_stepped.reshape(resident_members, channels, latitude_rows, longitude...  20.9 us
    unnamed x30, local copies, waits for them, and re-layouts  20.7 us
    convert_element_type x1, other arithmetic, on_device(): (grad_stepped + diffusivity[None, :, None, None] * grad_laplace).astype(j...  19.3 us
    add x4, other arithmetic, accumulate_member(): return running + softened_slope(own_values - partner_member)  18.3 us
    scatter-add x1, other arithmetic, on_device(): grad_stepped = grad_stepped.reshape(resident_members, PROGNOSTIC_COUNT, L...  16.4 us
  transfers between devices with their start and end apart: 10, of which 5 were waited for; matrix products, arithmetic and copies ran while one was open for 12% of the time, Pallas kernels for 0%

commit v1 on v0

--- a/solution.py
+++ b/solution.py
@@ -7,6 +7,28 @@
 LEVEL_COUNT = 37
 SCORED = 13
 DELTA = 0.1
+
+
+def in_order(tiles, dim):
+    tiles = jnp.moveaxis(tiles, 0, dim)
+    shape = tiles.shape
+    return tiles.reshape(*shape[:dim], shape[dim] * shape[dim + 1], *shape[dim + 2 :])
+
+
+def grow_blocks(array, axis):
+    peers = lax.axis_size(axis)
+    pieces = array[None]
+    for level in range(peers.bit_length() - 1):
+        apart = 1 << level
+        other = lax.ppermute(pieces, axis, [(i, i ^ apart) for i in range(peers)])
+        both = jnp.stack([pieces, other])
+        upper = lax.axis_index(axis) >> level & 1
+        pieces = jnp.where(upper == 0, both, both[::-1]).reshape(-1, *array.shape)
+    return pieces
+
+
+def collect(shard, axis, dim):
+    return in_order(grow_blocks(shard, axis), dim)
 
 
 def with_halo(block, sides, width):
@@ -97,7 +119,7 @@
     )
     observed_target = observed.reshape(evaluated_rows, latitude_rows, longitude_columns)
     own_values = member_prediction.astype(jnp.float32)
-    shard_values = lax.all_gather(member_prediction, "ens", axis=0, tiled=True).astype(jnp.float32)
+    shard_values = collect(member_prediction, "ens", 0).astype(jnp.float32)
 
     def accumulate_member(member_index, running):
         partner_member = lax.dynamic_index_in_dim(shard_values, member_index, 0, keepdims=False)

time: 463 us -> 449 us (0.970)
  other arithmetic: 106 us -> 92.6 us
  local copies, waits for them, and re-layouts: 110 us -> 123 us
  waiting for transfers between devices: 131 us -> 120 us
    all_gather x1 -> x0, waiting for transfers between devices: 36.1 us -> none  [on_device(): lax.all_gather(member_prediction, 'ens', axis=0, tiled=True)]
    ppermute x0 -> x1, waiting for transfers between devices: none -> 24.7 us  [grow_blocks(): other = lax.ppermute(pieces, axis, [(i, i ^ apart) for i in range(peers)])]
    add x4, other arithmetic: 18.3 us -> 6.38 us  [accumulate_member(): return running + softened_slope(own_values - partner_member)]
    while x0 -> x16, local copies, waits for them, and re-layouts: none -> 8.08 us
    convert_element_type x2 -> x1, other arithmetic: 7.99 us -> 3.17 us  [on_device(): shard_values = collect(member_prediction, 'ens', 0).astype(jnp.float32)]
    unnamed x30 -> x32, local copies, waits for them, and re-layouts: 20.7 us -> 21.9 us
  transfers between devices with their start and end apart: 10 -> 10, of which waited for: 5 -> 6; matrix products, arithmetic and copies ran while one was open for 12% -> 13% of each run, Pallas kernels for 0% -> 0%
where the time goes in v1:
time: 449 us; the launch traced here: 444 us
  local copies, waits for them, and re-layouts  123 us (27%)
  waiting for transfers between devices  120 us (27%)
  other arithmetic  92.6 us (21%)
  matrix products  41.2 us (9%)
  blocking collectives  40 us (9%)
  between operations  14.6 us (3%)
  starting transfers between devices  12.7 us (3%)
    psum x1, waiting for transfers between devices, on_device(): lax.psum((in_term, noise_term, mid_term, out_term, diffusivity_term), ('e...  91.4 us
    psum x1, blocking collectives, on_device(): lax.psum((in_term, noise_term, mid_term, out_term, diffusivity_term), ('e...  40 us
    ppermute x1, waiting for transfers between devices, grow_blocks(): other = lax.ppermute(pieces, axis, [(i, i ^ apart) for i in range(peers)])  24.7 us
    unnamed x32, local copies, waits for them, and re-layouts  21.9 us
    reshape x2, local copies, waits for them, and re-layouts, on_device(): grad_stepped.reshape(resident_members, channels, latitude_rows, longitude...  20.9 us
    convert_element_type x1, other arithmetic, on_device(): (grad_stepped + diffusivity[None, :, None, None] * grad_laplace).astype(j...  19.3 us
    scatter-add x1, other arithmetic, on_device(): grad_stepped = grad_stepped.reshape(resident_members, PROGNOSTIC_COUNT, L...  16.7 us
    transpose x1, local copies, waits for them, and re-layouts, on_device(): jnp.einsum('hc,mhn->mcn', input_weight, delta_first, preferred_element_ty...  11.6 us
  transfers between devices with their start and end apart: 10, of which 6 were waited for; matrix products, arithmetic and copies ran while one was open for 13% of the time, Pallas kernels for 0%

profile of v1, /device:TPU:0, one launch (start us, length us, event | category | flops | bytes accessed | tf_op | source)
XLA Modules:
  0.0 443.7 jit_solution(11544949695103647187)
XLA Ops:
  7.2 1.9 fusion.34
  9.1 2.5 collective-permute-start.1
  12.8 5.2 %fusion.27 = f32[2,4096,256]{2,1,0:T(8,128)} fusion(bf16[2,16,4096]{2,1,0:T(8,128)(2,1)S(1)} %reshape.84, bf16[256,16]{0,1:T(8,128)(2,1)} %param.14), kind=kOutput, calls=%fused_computation.70 | convolution fusion | flops 67108864 | bytes 8658944 | tf_op jit(solution)/shard_map/hk,mkn->mhn/dot_general | solution.py:100
  18.0 8.3 %copy.76 = bf16[2,222,32,128]{1,2,3,0:T(8,128)(2,1)} copy(bf16[2,222,32,128]{3,2,1,0:T(8,128)(2,1)} %param.10) | data formatting | bytes 7274496 | tf_op args[0]
  27.5 1.6 collective-permute-start.2
  29.1 2.5 collective-permute-start.3
  31.8 1.9 collective-permute-done.2
  34.1 4.8 %fusion.19 = f32[2,222,34,130]{1,2,3,0:T(8,128)S(1)} fusion(bf16[2,222,34,1]{1,2,3,0:T(8,128)(2,1)S(1)} %collective-permute-done.3, bf16[2,222,1,128]{1,2,3,0:T(2,128)(2,1)S(1)} %copy.81, bf16[2,222,32,128]{1,2,3,0:T(8,128)(2,1)} %copy.76, bf16[2,222,1,128]{1,2,3,0:T(2,128)(2,1)S(1)} %copy.79, bf16[2,222,34,1]{1,2,3,0:T(8,128)(2,1)S(1)} %collective-permute-done.2, ...), kind=kLoop, calls=%fused_computation.44 | loop fusion | flops 23549760 | bytes 11774948 | tf_op jit(solution)/shard_map/convert_element_type | solution.py:93
  39.0 11.2 %fusion.31 = (bf16[2,222,32,128]{1,2,3,0:T(8,128)(2,1)}, f32[2,222,32,128]{1,2,3,0:T(8,128)}, f32[2,222,32,128]{1,2,3,0:T(8,128)}) fusion(f32[222]{0:T(256)S(1)} %copy-done.13, bf16[2,222,32,128]{1,2,3,0:T(8,128)(2,1)} %copy.76, f32[2,222,34,130]{1,2,3,0:T(8,128)S(1)} %fusion.19), kind=kLoop, calls=%fused_computation.78 | loop fusion | flops 16367616 | bytes 50922360 | tf_op jit(solution)/shard_map/convert_element_type | solution.py:95
  50.1 8.3 %copy.83 = bf16[2,222,32,128]{3,2,1,0:T(8,128)(2,1)} copy(bf16[2,222,32,128]{1,2,3,0:T(8,128)(2,1)} %get-tuple-element.126) | data formatting | bytes 7274496 | tf_op jit(solution)/shard_map/convert_element_type | solution.py:95
  58.4 4.3 reshape.83
  62.7 10.1 %copy.82 = f32[2,222,32,128]{3,2,0,1:T(8,128)} copy(f32[2,222,32,128]{1,2,3,0:T(8,128)} %get-tuple-element.127) | data formatting | bytes 14548992 | tf_op jit(solution)/shard_map/add | solution.py:94
  72.8 9.9 %reshape.81 = f32[2,6,37,4096]{3,0,2,1:T(2,128)} reshape(f32[2,222,32,128]{3,2,0,1:T(8,128)} %copy.82) | data formatting | bytes 14548992 | tf_op jit(solution)/shard_map/reshape | solution.py:111
  82.8 2.2 slice.62
  85.6 7.3 %fusion.16 = (bf16[2,256,4096]{1,2,0:T(8,128)(2,1)S(1)}, f32[2,4096,256]{2,1,0:T(8,128)}) fusion(f32[2,4096,256]{2,1,0:T(8,128)} %fusion.27, bf16[2,222,4096]{2,1,0:T(8,128)(2,1)S(1)} %copy-done.9, bf16[256,222]{0,1:T(8,128)(2,1)S(1)} %copy-done.11), kind=kOutput, calls=%fused_computation.37 | convolution fusion | flops 943718400 | bytes 24722432 | tf_op jit(solution)/shard_map/hc,mcn->mhn/dot_general | solution.py:97
  93.0 4.6 %fusion.10 = (bf16[2,256,4096]{1,2,0:T(8,128)(2,1)S(1)}, f32[2,4096,256]{2,1,0:T(8,128)}) fusion(bf16[2,256,4096]{1,2,0:T(8,128)(2,1)S(1)} %get-tuple-element.139, bf16[256,256]{1,0:T(8,128)(2,1)S(1)} %copy-done), kind=kOutput, calls=%fused_computation.28 | convolution fusion | flops 1084227584 | bytes 16908288 | tf_op jit(solution)/shard_map/hk,mkn->mhn/dot_general | solution.py:104
  97.6 2.0 copy-done.5
  99.6 2.0 fusion.21
  101.6 1.6 broadcast_in_dim_reshape.4
  103.2 1.5 collective-permute-start.4
  104.7 1.6 stack_broadcast_in_dim_reshape.3
  106.3 2.3 reshape.91
  108.5 24.7 %collective-permute-done.4 = bf16[1,2,78,32,128]{4,3,2,1,0:T(8,128)(2,1)} collective-permute-done((bf16[1,2,78,32,128]{4,3,2,1,0:T(8,128)(2,1)}, bf16[1,2,78,32,128]{4,3,2,1,0:T(8,128)(2,1)}, u32[]{:S(2)}, u32[]{:S(2)}) %collective-permute-start.4) | collective-permute-done | bytes 1277984 | tf_op jit(solution)/shard_map/ppermute | solution.py:23
  133.2 1.9 pad_maximum_fusion
  135.7 3.2 bitcast_convert_fusion
  138.8 20.7 %while.14 = (s32[]{:T(128)}, f32[2,78,32,128]{3,2,1,0:T(8,128)}, f32[4,78,32,128]{3,2,1,0:T(8,128)}, f32[2,78,32,128]{3,2,1,0:T(8,128)S(1)}, s32[]{:T(128)}, /*index=5*/s32[]{:T(128)}) while((s32[]{:T(128)}, f32[2,78,32,128]{3,2,1,0:T(8,128)}, f32[4,78,32,128]{3,2,1,0:T(8,128)}, f32[2,78,32,128]{3,2,1,0:T(8,128)S(1)}, s32[]{:T(128)}, ...), condition=%wide.region_1.2_spmd.clone, body=%wide.region_0.1_spmd.clone.sunk | while | flops 3833859 | bytes 31948948 | solution.py:128
  138.8 1.5 dynamic-slice_bitcast_fusion.2
  140.9 1.6 select_add_fusion.2
  142.5 1.5 copy-done.2
  144.0 1.5 dynamic-slice_bitcast_fusion.2
  146.1 1.6 select_add_fusion.2
  147.7 1.5 copy-done.2
  149.2 1.5 dynamic-slice_bitcast_fusion.2
  151.3 1.6 select_add_fusion.2
  152.9 1.5 copy-done.2
  154.4 1.5 dynamic-slice_bitcast_fusion.2
  156.5 1.6 select_add_fusion.2
  158.1 1.5 copy-done.2
  159.5 3.9 subtract_convert_fusion
  163.5 1.8 reshape.87
  165.2 3.2 convolution_bitcast_fusion.4
  168.4 6.4 %fusion.6 = bf16[2,256,4096]{1,2,0:T(8,128)(2,1)S(1)} fusion(f32[2,4096,256]{2,1,0:T(8,128)} %get-tuple-element.142, bf16[2,78,4096]{2,1,0:T(8,128)(2,1)S(1)} %reshape.87, bf16[78,256,1]{1,0,2:T(8,128)(2,1)S(1)} %reshape.113), kind=kOutput, calls=%fused_computation.21 | convolution fusion | flops 346030080 | bytes 13900800 | tf_op jit(solution)/shard_map/ch,mcn->mhn/dot_general | solution.py:139
  174.9 2.0 convolution_bitcast_fusion.2
  176.9 3.5 fusion.5
  180.5 1.8 convolution_bitcast_fusion.3
  183.9 4.4 convolution_bitcast_fusion
  188.4 2.4 reshape.95
  190.8 1.9 copy.89
  192.7 11.6 %copy.87 = f32[2,222,4096]{2,0,1:T(2,128)} copy(f32[2,222,4096]{2,1,0:T(8,128)} %convolution_bitcast_fusion) | data formatting | bytes 14548992 | tf_op jit(solution)/shard_map/hc,mhn->mcn/transpose | solution.py:156
  204.3 16.7 %scatter_fusion = f32[2,6,37,4096]{3,0,2,1:T(2,128)} fusion(f32[2,6,37,4096]{3,0,2,1:T(2,128)} %bitcast.134, s32[13]{0:T(128)S(1)} %multiply_bitcast_fusion, f32[13,2,6,4096]{3,1,2,0:T(2,128)S(1)} %copy.89), kind=kCustom, calls=%fused_computation | custom fusion | flops 638976 | bytes 7667764 | tf_op jit(solution)/shard_map/scatter-add | solution.py:162
  221.0 10.8 %reshape.89 = f32[2,222,32,128]{3,2,0,1:T(8,128)} reshape(f32[2,6,37,4096]{3,0,2,1:T(2,128)} %scatter_fusion) | data formatting | bytes 14548992 | tf_op jit(solution)/shard_map/reshape | solution.py:166
  231.9 10.1 %copy.96 = f32[2,222,32,128]{1,2,3,0:T(8,128)} copy(f32[2,222,32,128]{3,2,0,1:T(8,128)} %reshape.89) | data formatting | bytes 14548992 | tf_op jit(solution)/shard_map/reshape | solution.py:166
  241.9 9.9 %multiply_reduce_fusion = (f32[222]{0:T(256)S(1)}, bf16[2,222,32,128]{1,2,3,0:T(8,128)(2,1)S(1)}) fusion(f32[2,222,32,128]{1,2,3,0:T(8,128)} %copy.96, f32[2,222,32,128]{1,2,3,0:T(8,128)} %get-tuple-element.128), kind=kLoop, calls=%fused_computation.40 | loop fusion | flops 5455650 | bytes 18187128 | tf_op jit(solution)/shard_map/reduce_sum | solution.py:169
  251.9 2.0 copy-done.3
  255.2 40.0 %all-reduce = (f32[256,16]{0,1:T(8,128)S(1)}, f32[222]{0:T(256)S(1)}) all-reduce(f32[256,16]{0,1:T(8,128)S(1)} %convolution_bitcast_fusion.5, f32[222]{0:T(256)S(1)} %get-tuple-element.129), channel_id=1, replica_groups=mesh['ens'=2,'lat'=4,'lon'=4] {'ens','lat','lon'}, use_global_device_ids=true, to_apply=%region_4.5 | all-reduce | flops 4318 | bytes 34544 | tf_op jit(solution)/shard_map/psum | solution.py:170
  297.0 2.2 collective-permute-start.7
  299.2 1.7 collective-permute-start.8
  303.3 8.6 %convert_multiply_fusion = f32[2,222,34,130]{1,2,3,0:T(8,128)} fusion(bf16[2,222,34,1]{1,2,3,0:T(8,128)(2,1)S(1)} %collective-permute-done.8, bf16[2,222,1,128]{1,2,3,0:T(2,128)(2,1)S(1)} %copy.94, bf16[2,222,32,128]{1,2,3,0:T(8,128)(2,1)} %copy-done.3, bf16[2,222,1,128]{1,2,3,0:T(2,128)(2,1)S(1)} %copy.93, ...), kind=kLoop, calls=%fused_computation.4 | loop fusion | flops 21587280 | bytes 11775016 | tf_op jit(solution)/shard_map/mul | solution.py:64
  311.9 19.3 %fusion.4 = bf16[2,222,32,128]{1,2,3,0:T(8,128)(2,1)} fusion(f32[2,222,32,128]{1,2,3,0:T(8,128)} %copy.96, f32[2,222,34,130]{1,2,3,0:T(8,128)} %convert_multiply_fusion, f32[222]{0:T(256)S(1)} %copy-done.13), kind=kLoop, calls=%fused_computation.12 | loop fusion | flops 14548992 | bytes 40010616 | tf_op jit(solution)/shard_map/convert_element_type | solution.py:179
  331.1 8.3 %copy.105 = bf16[2,222,32,128]{3,2,1,0:T(8,128)(2,1)} copy(bf16[2,222,32,128]{1,2,3,0:T(8,128)(2,1)} %fusion.4) | data formatting | bytes 7274496
  339.4 91.4 %all-reduce.4.cloned.1.call-done = (f32[256,222]{0,1:T(8,128)}, f32[256,256]{1,0:T(8,128)}, f32[6,13,256]{2,0,1:T(8,128)}) async-done(((f32[256,222]{0,1:T(8,128)}, f32[256,256]{1,0:T(8,128)}, f32[6,13,256]{2,0,1:T(8,128)}), (f32[256,222]{0,1:T(8,128)}, f32[256,256]{1,0:T(8,128)}, f32[6,13,256]{2,0,1:T(8,128)})) %all-reduce.4.cloned.1.call-update) | async-done | bytes 569360 | tf_op jit(solution)/shard_map/psum | solution.py:170
  430.9 1.7 scatter_fusion.1
  433.3 1.6 broadcast_multiply_fusion.1
  435.0 1.7 broadcast_multiply_fusion
  (80 shorter events, 14.4 us)
Async XLA Ops:
  7.2 85.8 %copy-start = (bf16[256,256]{1,0:T(8,128)(2,1)S(1)}, bf16[256,256]{1,0:T(8,128)(2,1)}, u32[]{:S(2)}) copy-start(bf16[256,256]{1,0:T(8,128)(2,1)} %param.15) | copy-start | bytes 393220
  7.2 423.7 %all-reduce.4.cloned.1.call-start = ((), (), s32[]{:S(2)}) async-start(), calls=%async_computation | async-start | bytes 1196032 | tf_op jit(solution)/shard_map/psum | solution.py:170
  9.1 17.4 %collective-permute-start.1 = (bf16[2,222,1,128]{3,1,2,0:T(8,128)(2,1)S(1)}, bf16[2,222,1,128]{3,1,2,0:T(8,128)(2,1)S(1)}, u32[]{:S(2)}, u32[]{:S(2)}) collective-permute-start(bf16[2,222,1,128]{3,1,2,0:T(8,128)(2,1)S(1)} %copy.114), channel_id=1, source_target_pairs={{4,0},{8,4},{12,8},{0,12},{5,1},{9,5},{13,9},{1,13},{6,2},{10,6},{... | collective-permute-start | bytes 341000 | tf_op jit(solution)/shard_map/ppermute | solution.py:43
  11.6 14.6 %collective-permute-start = (bf16[2,222,1,128]{3,1,2,0:T(8,128)(2,1)S(1)}, bf16[2,222,1,128]{3,1,2,0:T(8,128)(2,1)S(1)}, u32[]{:S(2)}, u32[]{:S(2)}) collective-permute-start(bf16[2,222,1,128]{3,1,2,0:T(8,128)(2,1)S(1)} %copy.113), channel_id=1, source_target_pairs={{0,4},{4,8},{8,12},{12,0},{1,5},{5,9},{9,13},{13,1},{2,6},{6,10},{... | collective-permute-start | bytes 341000 | tf_op jit(solution)/shard_map/ppermute | solution.py:40
  26.3 5.4 %copy-start.12 = (bf16[222,256]{1,0:T(8,128)(2,1)S(1)}, bf16[222,256]{1,0:T(8,128)(2,1)}, u32[]{:S(2)}) copy-start(bf16[222,256]{1,0:T(8,128)(2,1)} %param.16) | copy-start | bytes 340996
  27.5 6.2 %collective-permute-start.2 = (bf16[2,222,34,1]{1,2,3,0:T(8,128)(2,1)S(1)}, bf16[2,222,34,1]{1,2,3,0:T(8,128)(2,1)S(1)}, u32[]{:S(2)}, u32[]{:S(2)}) collective-permute-start(bf16[2,222,34,1]{1,2,3,0:T(8,128)(2,1)S(1)} %get-tuple-element.133), channel_id=1, source_target_pairs={{0,1},{1,2},{2,3},{3,0},{4,5},{5,6},{6,7},{7,4},{8,9},{9,10},{10,1... | collective-permute-start | bytes 90584 | tf_op jit(solution)/shard_map/ppermute | solution.py:40
  29.1 5.0 %collective-permute-start.3 = (bf16[2,222,34,1]{1,2,3,0:T(8,128)(2,1)S(1)}, bf16[2,222,34,1]{1,2,3,0:T(8,128)(2,1)S(1)}, u32[]{:S(2)}, u32[]{:S(2)}) collective-permute-start(bf16[2,222,34,1]{1,2,3,0:T(8,128)(2,1)S(1)} %get-tuple-element.134), channel_id=1, source_target_pairs={{1,0},{2,1},{3,2},{0,3},{5,4},{6,5},{7,6},{4,7},{9,8},{10,9},{11,1... | collective-permute-start | bytes 90584 | tf_op jit(solution)/shard_map/ppermute | solution.py:43
  31.8 7.2 %copy-start.13 = (f32[222]{0:T(256)S(1)}, f32[222]{0:T(256)}, u32[]{:S(2)}) copy-start(f32[222]{0:T(256)} %param.17) | copy-start | bytes 2668
  82.8 2.8 copy-start.9
  82.8 2.8 copy-start.11
  93.0 4.6 %copy-start.6 = (bf16[2,256,4096]{1,2,0:T(8,128)(2,1)}, bf16[2,256,4096]{1,2,0:T(8,128)(2,1)S(1)}, u32[]{:S(2)}) copy-start(bf16[2,256,4096]{1,2,0:T(8,128)(2,1)S(1)} %get-tuple-element.139) | copy-start | bytes 12582916
  97.6 2.0 copy-start.5
  101.6 3.1 copy-start.4
  103.2 30.0 %collective-permute-start.4 = (bf16[1,2,78,32,128]{4,3,2,1,0:T(8,128)(2,1)}, bf16[1,2,78,32,128]{4,3,2,1,0:T(8,128)(2,1)}, u32[]{:S(2)}, u32[]{:S(2)}) collective-permute-start(bf16[1,2,78,32,128]{4,3,2,1,0:T(8,128)(2,1)} %broadcast_in_dim_reshape.4), channel_id=1, source_target_pairs={{0,16},{16,0},{1,17},{17,1},{2,18},{18,2},{3,19},{19,3},{4,20},{20... | collective-permute-start | bytes 3833864 | tf_op jit(solution)/shard_map/ppermute | solution.py:23
  138.8 2.1 copy-start.1
  142.5 1.5 copy-start.2
  144.0 2.1 copy-start.1
  147.7 1.5 copy-start.2
  149.2 2.1 copy-start.1
  152.9 1.5 copy-start.2
  154.4 2.1 copy-start.1
  158.1 1.5 copy-start.2
  165.2 11.7 %slice-start = ((s8[8388608]{0:T(1024)(128)(4,1)}), s8[4194304]{0:T(1024)(128)(4,1)S(1)}, s32[]{:S(2)}) async-start(s8[8388608]{0:T(1024)(128)(4,1)} %bitcast.139), calls=%async_computation.1 | async-start | bytes 8388608
  168.4 6.5 %copy-start.7 = (bf16[2,256,4096]{1,2,0:T(8,128)(2,1)S(1)}, bf16[2,256,4096]{1,2,0:T(8,128)(2,1)}, u32[]{:S(2)}) copy-start(bf16[2,256,4096]{1,2,0:T(8,128)(2,1)} %copy-done.6) | copy-start | bytes 12582916
  168.4 8.5 %slice-start.1 = ((s8[8388608]{0:T(1024)(128)(4,1)}), s8[4194304]{0:T(1024)(128)(4,1)S(1)}, s32[]{:S(2)}) async-start(s8[8388608]{0:T(1024)(128)(4,1)} %bitcast.139), calls=%async_computation.2 | async-start | bytes 8388608
  176.9 3.6 copy-start.10
  182.3 1.3 copy-start.8
  251.9 2.0 copy-start.3
  254.6 41.4 %collective-permute-start.6 = (bf16[2,222,1,128]{3,1,2,0:T(8,128)(2,1)S(1)}, bf16[2,222,1,128]{3,1,2,0:T(8,128)(2,1)S(1)}, u32[]{:S(2)}, u32[]{:S(2)}) collective-permute-start(bf16[2,222,1,128]{3,1,2,0:T(8,128)(2,1)S(1)} %copy.92), channel_id=1, source_target_pairs={{4,0},{8,4},{12,8},{0,12},{5,1},{9,5},{13,9},{1,13},{6,2},{10,6},{... | collective-permute-start | bytes 341000 | tf_op jit(solution)/shard_map/ppermute | solution.py:43
  255.0 40.8 %collective-permute-start.5 = (bf16[2,222,1,128]{3,1,2,0:T(8,128)(2,1)S(1)}, bf16[2,222,1,128]{3,1,2,0:T(8,128)(2,1)S(1)}, u32[]{:S(2)}, u32[]{:S(2)}) collective-permute-start(bf16[2,222,1,128]{3,1,2,0:T(8,128)(2,1)S(1)} %copy.91), channel_id=1, source_target_pairs={{0,4},{4,8},{8,12},{12,0},{1,5},{5,9},{9,13},{13,1},{2,6},{6,10},{... | collective-permute-start | bytes 341000 | tf_op jit(solution)/shard_map/ppermute | solution.py:40
  297.0 5.9 %collective-permute-start.7 = (bf16[2,222,34,1]{1,2,3,0:T(8,128)(2,1)S(1)}, bf16[2,222,34,1]{1,2,3,0:T(8,128)(2,1)S(1)}, u32[]{:S(2)}, u32[]{:S(2)}) collective-permute-start(bf16[2,222,34,1]{1,2,3,0:T(8,128)(2,1)S(1)} %get-tuple-element.131), channel_id=1, source_target_pairs={{0,1},{1,2},{2,3},{3,0},{4,5},{5,6},{6,7},{7,4},{8,9},{9,10},{10,1... | collective-permute-start | bytes 90584 | tf_op jit(solution)/shard_map/ppermute | solution.py:40
  299.2 4.1 collective-permute-start.8
Sparse Core Ops, SparseCore 0:
  302.3 128.4 all-reduce.3
